TPU v7x, 32 devices: a whole 2x2x4 slice. The times are simulated.
32 devices in a mesh: segment: 4 (over y, x), col: 8 (over z, core).
Axes of the slice: x: 2, y: 2, z: 4, core: 2. Of those that a mesh axis runs over, the one named last changes fastest.
Arguments:
- left_env: bfloat16 [384, 8192], P(None, 'col'), may hold values from -6 to 6
- bit_strings: int32 [384, 4], P(None, 'segment'), may hold values from 0 to 1
- site_tensors: bfloat16 [4, 2, 8192, 8192], P('segment', None, None, 'col'), may hold values from -0.0625 to 0.0625
Outputs:
- section_env: bfloat16 [4, 384, 8192], P('segment', None, 'col')
- section_log: float32 [4, 384], P('segment')
All inputs are finite; a program needn't handle non-finite values. Where the computation divides by a largest or mean magnitude, that divisor is 1e-20 or more.
Results may differ from a plain program's by a relative error of at most 0.0065.
Values may be sent and summed in bfloat16 or wider, within the bound.
A program may use at most 128 MiB of HBM per device.

v0:
```python
import jax
import jax.numpy as jnp
from jax import lax
from jax.sharding import PartitionSpec as P

MICRO = 2
epsilon = 1e-06


def passed_along(value, axis, by):
    length = lax.axis_size(axis)
    pairs = [(i, i + by) for i in range(length) if 0 <= i + by < length]
    return lax.ppermute(value, axis, pairs)


def advance(vector, bit_column, tensor):
    batch_rows = vector.shape[0]
    col_width = tensor.shape[2]
    block = min(128, batch_rows)
    buffer_rows = (batch_rows + block - 1 + block - 1) // block * block
    block_count = buffer_rows // block
    ones_before = jnp.cumsum(bit_column) - bit_column
    index_rows = jnp.arange(batch_rows, dtype=jnp.int32)
    zeros_before = index_rows - ones_before
    zero_count = batch_rows - jnp.sum(bit_column)
    start_one = (zero_count + block - 1) // block * block
    slot = jnp.where(bit_column == 1, start_one + ones_before, zeros_before)
    source = jnp.zeros((buffer_rows,), jnp.int32).at[slot].set(index_rows)
    filled = jnp.zeros((buffer_rows,), jnp.bool_).at[slot].set(True)
    block_bit = (jnp.arange(block_count, dtype=jnp.int32) * block >= start_one).astype(jnp.int32)
    arranged_in = jnp.where(
        filled[:, None], jnp.take(vector, source, axis=0), jnp.zeros((), vector.dtype)
    )
    gathered_piece = lax.all_gather(arranged_in, "col", axis=1, tiled=True)
    width = gathered_piece.shape[1]
    pieces = gathered_piece.reshape(block_count, block, width)

    def one_block(inputs):
        rows_block, bit_value = inputs
        weight_block = lax.dynamic_slice(
            tensor, (bit_value, 0, jnp.int32(0)), (1, width, col_width)
        )[0]
        return jnp.dot(rows_block, weight_block, preferred_element_type=jnp.float32)

    result = lax.map(one_block, (pieces, block_bit))
    arranged_out = result.reshape(buffer_rows, col_width)
    chosen = jnp.take(arranged_out, slot, axis=0)
    maximum = lax.pmax(jnp.max(jnp.abs(chosen), axis=1), "col") + epsilon
    return ((chosen / maximum[:, None]).astype(jnp.bfloat16), jnp.log(maximum))


def local(left_env, bit_strings, site_tensors):
    segment_count = lax.axis_size("segment")
    segment_index = lax.axis_index("segment")
    row_count = left_env.shape[0]
    col_width = left_env.shape[1]
    granules = 2 * MICRO
    batch_rows = row_count // granules
    env_out = jnp.zeros((row_count, col_width), jnp.bfloat16)
    log_out = jnp.zeros((row_count,), jnp.float32)
    incoming = jnp.zeros((batch_rows, col_width), jnp.bfloat16)
    tick_total = granules + segment_count - 1
    for tick_step in range(tick_total):
        position = tick_step - segment_index
        active = (position >= 0) & (position < granules)
        offset_rows = jnp.clip(position, 0, granules - 1) * batch_rows
        from_input = lax.dynamic_slice_in_dim(left_env, offset_rows, batch_rows, 0)
        current = jnp.where(segment_index == 0, from_input, incoming)
        bit_block = lax.dynamic_slice_in_dim(bit_strings, offset_rows, batch_rows, 0)
        current, logs_site = advance(current, bit_block[:, 0], site_tensors[0])
        old_env = lax.dynamic_slice_in_dim(env_out, offset_rows, batch_rows, 0)
        old_log = lax.dynamic_slice_in_dim(log_out, offset_rows, batch_rows, 0)
        env_out = lax.dynamic_update_slice_in_dim(
            env_out, jnp.where(active, current, old_env), offset_rows, 0
        )
        log_out = lax.dynamic_update_slice_in_dim(
            log_out, jnp.where(active, logs_site, old_log), offset_rows, 0
        )
        if tick_step + 1 < tick_total:
            incoming = passed_along(current, "segment", 1)
    return (env_out[None], log_out[None])


def solution(mesh):
    placed = (P(None, "col"), P(None, "segment"), P("segment", None, None, "col"))
    return jax.shard_map(
        local,
        mesh=mesh,
        in_specs=placed,
        out_specs=(P("segment", None, "col"), P("segment", None)),
        check_vma=False,
    )
```

profile of v0, /device:TPU:0, one launch (start us, length us, event | category | flops | bytes accessed | tf_op | source)
XLA Modules:
  0.0 615.0 jit_solution(9324668334376139181)
XLA Ops:
  7.2 1.7 fusion.162
  17.8 38.0 %all-gather.8.cloned.1.call-done = bf16[192,8192]{1,0:T(8,128)(2,1)} async-done(((bf16[192,1024]{1,0:T(8,128)(2,1)}), bf16[192,8192]{1,0:T(8,128)(2,1)}) %all-gather.8.cloned.1.call-update) | async-done | bytes 3145744 | tf_op jit(solution)/shard_map/all_gather | solution.py:34
  56.0 23.1 %while.70 = (s32[]{:T(128)}, f32[2,96,1024]{2,1,0:T(8,128)S(1)}, bf16[2,96,8192]{2,1,0:T(8,128)(2,1)}, s32[2]{0:T(128)S(1)}, bf16[2,8192,1024]{2,1,0:T(8,128)(2,1)}, /*index=5*/s32[]{:T(128)}, s32[]{:T(128)}, s32[]{:T(128)}) while((s32[]{:T(128)}, f32[2,96,1024]{2,1,0:T(8,128)S(1)}, bf16[2,96,8192]{2,1,0:T(8,128)(2,1)}, s32[2]{0:T(128)S(1)}, ...), condition=%wide.region_5.7_spmd, body=%wide.region_4.6_spmd.sunk | while | flops 1610612736 | bytes 18744456 | solution.py:45
  58.5 9.0 %fusion.192 = f32[2,96,1024]{2,1,0:T(8,128)S(1)} fusion(f32[2,96,1024]{2,1,0:T(8,128)S(1)} %get-tuple-element.582, s32[]{:T(128)} %get-tuple-element.581, bf16[2,8192,1024]{2,1,0:T(8,128)(2,1)} %get-tuple-element.593, s32[]{:T(128)S(6)} %select_n.653, bf16[2,96,8192]{2,1,0:T(8,128)(2,1)} %get-tuple-element.591), kind=kOutput, calls=%fused_computation.34.clone.1 | convolution fusion | flops 1610612736 | bytes 18744324 | tf_op jit(solution)/shard_map/while/body/eval_jaxpr/dot_general | solution.py:43
  70.1 9.0 %fusion.192 = f32[2,96,1024]{2,1,0:T(8,128)S(1)} fusion(f32[2,96,1024]{2,1,0:T(8,128)S(1)} %get-tuple-element.582, s32[]{:T(128)} %get-tuple-element.581, bf16[2,8192,1024]{2,1,0:T(8,128)(2,1)} %get-tuple-element.593, s32[]{:T(128)S(6)} %select_n.653, bf16[2,96,8192]{2,1,0:T(8,128)(2,1)} %get-tuple-element.591), kind=kOutput, calls=%fused_computation.34.clone.1 | convolution fusion | flops 1610612736 | bytes 18744324 | tf_op jit(solution)/shard_map/while/body/eval_jaxpr/dot_general | solution.py:43
  80.1 14.7 %pmax.49 = f32[96]{0:T(128)S(1)} all-reduce(f32[96]{0:T(128)S(1)} %abs_reduce_fusion.6), channel_id=1, replica_groups=mesh['segment'=4,'col'=8] {'col'}, use_global_device_ids=true, to_apply=%region_7.10 | all-reduce | flops 96 | bytes 768 | tf_op jit(solution)/shard_map/pmax | solution.py:48
  95.1 3.4 collective-permute-start
  98.6 3.1 collective-permute-done
  106.8 34.4 %all-gather.10.cloned.1.call-done = bf16[192,8192]{1,0:T(8,128)(2,1)} async-done(((bf16[192,1024]{1,0:T(8,128)(2,1)}), bf16[192,8192]{1,0:T(8,128)(2,1)}) %all-gather.10.cloned.1.call-update) | async-done | bytes 3145744 | tf_op jit(solution)/shard_map/all_gather | solution.py:34
  141.3 23.1 %while.71 = (s32[]{:T(128)}, f32[2,96,1024]{2,1,0:T(8,128)S(1)}, bf16[2,96,8192]{2,1,0:T(8,128)(2,1)}, s32[2]{0:T(128)S(1)}, bf16[2,8192,1024]{2,1,0:T(8,128)(2,1)}, /*index=5*/s32[]{:T(128)}, s32[]{:T(128)}, s32[]{:T(128)}) while((s32[]{:T(128)}, f32[2,96,1024]{2,1,0:T(8,128)S(1)}, bf16[2,96,8192]{2,1,0:T(8,128)(2,1)}, s32[2]{0:T(128)S(1)}, ...), condition=%wide.region_13.16_spmd, body=%wide.region_12.15_spmd.sunk | while | flops 1610612736 | bytes 18744456 | solution.py:45
  143.8 9.0 %fusion.195 = f32[2,96,1024]{2,1,0:T(8,128)S(1)} fusion(f32[2,96,1024]{2,1,0:T(8,128)S(1)} %get-tuple-element.606, s32[]{:T(128)} %get-tuple-element.605, bf16[2,8192,1024]{2,1,0:T(8,128)(2,1)} %get-tuple-element.617, s32[]{:T(128)S(6)} %select_n.654, bf16[2,96,8192]{2,1,0:T(8,128)(2,1)} %get-tuple-element.615), kind=kOutput, calls=%fused_computation.42.clone.1 | convolution fusion | flops 1610612736 | bytes 18744324 | tf_op jit(solution)/shard_map/while/body/eval_jaxpr/dot_general | solution.py:43
  155.4 9.0 %fusion.195 = f32[2,96,1024]{2,1,0:T(8,128)S(1)} fusion(f32[2,96,1024]{2,1,0:T(8,128)S(1)} %get-tuple-element.606, s32[]{:T(128)} %get-tuple-element.605, bf16[2,8192,1024]{2,1,0:T(8,128)(2,1)} %get-tuple-element.617, s32[]{:T(128)S(6)} %select_n.654, bf16[2,96,8192]{2,1,0:T(8,128)(2,1)} %get-tuple-element.615), kind=kOutput, calls=%fused_computation.42.clone.1 | convolution fusion | flops 1610612736 | bytes 18744324 | tf_op jit(solution)/shard_map/while/body/eval_jaxpr/dot_general | solution.py:43
  165.4 14.8 %pmax.50 = f32[96]{0:T(128)S(1)} all-reduce(f32[96]{0:T(128)S(1)} %abs_reduce_fusion.5), channel_id=1, replica_groups=mesh['segment'=4,'col'=8] {'col'}, use_global_device_ids=true, to_apply=%region_15.18 | all-reduce | flops 96 | bytes 768 | tf_op jit(solution)/shard_map/pmax | solution.py:48
  180.4 3.6 collective-permute-start.1
  184.0 3.0 collective-permute-done.1
  191.8 34.7 %all-gather.12.cloned.1.call-done = bf16[192,8192]{1,0:T(8,128)(2,1)} async-done(((bf16[192,1024]{1,0:T(8,128)(2,1)}), bf16[192,8192]{1,0:T(8,128)(2,1)}) %all-gather.12.cloned.1.call-update) | async-done | bytes 3145744 | tf_op jit(solution)/shard_map/all_gather | solution.py:34
  226.6 23.1 %while.72 = (s32[]{:T(128)}, f32[2,96,1024]{2,1,0:T(8,128)S(1)}, bf16[2,96,8192]{2,1,0:T(8,128)(2,1)}, s32[2]{0:T(128)S(1)}, bf16[2,8192,1024]{2,1,0:T(8,128)(2,1)}, /*index=5*/s32[]{:T(128)}, s32[]{:T(128)}, s32[]{:T(128)}) while((s32[]{:T(128)}, f32[2,96,1024]{2,1,0:T(8,128)S(1)}, bf16[2,96,8192]{2,1,0:T(8,128)(2,1)}, s32[2]{0:T(128)S(1)}, ...), condition=%wide.region_21.24_spmd, body=%wide.region_20.23_spmd.sunk | while | flops 1610612736 | bytes 18744456 | solution.py:45
  229.1 9.0 %fusion.198 = f32[2,96,1024]{2,1,0:T(8,128)S(1)} fusion(f32[2,96,1024]{2,1,0:T(8,128)S(1)} %get-tuple-element.630, s32[]{:T(128)} %get-tuple-element.629, bf16[2,8192,1024]{2,1,0:T(8,128)(2,1)} %get-tuple-element.641, s32[]{:T(128)S(6)} %select_n.655, bf16[2,96,8192]{2,1,0:T(8,128)(2,1)} %get-tuple-element.639), kind=kOutput, calls=%fused_computation.50.clone.1 | convolution fusion | flops 1610612736 | bytes 18744324 | tf_op jit(solution)/shard_map/while/body/eval_jaxpr/dot_general | solution.py:43
  240.7 9.0 %fusion.198 = f32[2,96,1024]{2,1,0:T(8,128)S(1)} fusion(f32[2,96,1024]{2,1,0:T(8,128)S(1)} %get-tuple-element.630, s32[]{:T(128)} %get-tuple-element.629, bf16[2,8192,1024]{2,1,0:T(8,128)(2,1)} %get-tuple-element.641, s32[]{:T(128)S(6)} %select_n.655, bf16[2,96,8192]{2,1,0:T(8,128)(2,1)} %get-tuple-element.639), kind=kOutput, calls=%fused_computation.50.clone.1 | convolution fusion | flops 1610612736 | bytes 18744324 | tf_op jit(solution)/shard_map/while/body/eval_jaxpr/dot_general | solution.py:43
  250.6 14.7 %pmax.51 = f32[96]{0:T(128)S(1)} all-reduce(f32[96]{0:T(128)S(1)} %abs_reduce_fusion.4), channel_id=1, replica_groups=mesh['segment'=4,'col'=8] {'col'}, use_global_device_ids=true, to_apply=%region_23.26 | all-reduce | flops 96 | bytes 768 | tf_op jit(solution)/shard_map/pmax | solution.py:48
  265.7 3.4 collective-permute-start.2
  269.1 3.1 collective-permute-done.2
  277.4 34.3 %all-gather.14.cloned.1.call-done = bf16[192,8192]{1,0:T(8,128)(2,1)} async-done(((bf16[192,1024]{1,0:T(8,128)(2,1)}), bf16[192,8192]{1,0:T(8,128)(2,1)}) %all-gather.14.cloned.1.call-update) | async-done | bytes 3145744 | tf_op jit(solution)/shard_map/all_gather | solution.py:34
  311.8 23.1 %while.73 = (s32[]{:T(128)}, f32[2,96,1024]{2,1,0:T(8,128)S(1)}, bf16[2,96,8192]{2,1,0:T(8,128)(2,1)}, s32[2]{0:T(128)S(1)}, bf16[2,8192,1024]{2,1,0:T(8,128)(2,1)}, /*index=5*/s32[]{:T(128)}, s32[]{:T(128)}, s32[]{:T(128)}) while((s32[]{:T(128)}, f32[2,96,1024]{2,1,0:T(8,128)S(1)}, bf16[2,96,8192]{2,1,0:T(8,128)(2,1)}, s32[2]{0:T(128)S(1)}, ...), condition=%wide.region_29.32_spmd, body=%wide.region_28.31_spmd.sunk | while | flops 1610612736 | bytes 18744456 | solution.py:45
  314.4 9.0 %fusion.201 = f32[2,96,1024]{2,1,0:T(8,128)S(1)} fusion(f32[2,96,1024]{2,1,0:T(8,128)S(1)} %get-tuple-element.654, s32[]{:T(128)} %get-tuple-element.653, bf16[2,8192,1024]{2,1,0:T(8,128)(2,1)} %get-tuple-element.665, s32[]{:T(128)S(6)} %select_n.656, bf16[2,96,8192]{2,1,0:T(8,128)(2,1)} %get-tuple-element.663), kind=kOutput, calls=%fused_computation.58.clone.1 | convolution fusion | flops 1610612736 | bytes 18744324 | tf_op jit(solution)/shard_map/while/body/eval_jaxpr/dot_general | solution.py:43
  325.9 9.0 %fusion.201 = f32[2,96,1024]{2,1,0:T(8,128)S(1)} fusion(f32[2,96,1024]{2,1,0:T(8,128)S(1)} %get-tuple-element.654, s32[]{:T(128)} %get-tuple-element.653, bf16[2,8192,1024]{2,1,0:T(8,128)(2,1)} %get-tuple-element.665, s32[]{:T(128)S(6)} %select_n.656, bf16[2,96,8192]{2,1,0:T(8,128)(2,1)} %get-tuple-element.663), kind=kOutput, calls=%fused_computation.58.clone.1 | convolution fusion | flops 1610612736 | bytes 18744324 | tf_op jit(solution)/shard_map/while/body/eval_jaxpr/dot_general | solution.py:43
  335.9 14.7 %pmax.52 = f32[96]{0:T(128)S(1)} all-reduce(f32[96]{0:T(128)S(1)} %abs_reduce_fusion.3), channel_id=1, replica_groups=mesh['segment'=4,'col'=8] {'col'}, use_global_device_ids=true, to_apply=%region_31.34 | all-reduce | flops 96 | bytes 768 | tf_op jit(solution)/shard_map/pmax | solution.py:48
  351.0 3.4 collective-permute-start.3
  354.4 3.1 collective-permute-done.3
  362.6 34.4 %all-gather.16.cloned.1.call-done = bf16[192,8192]{1,0:T(8,128)(2,1)} async-done(((bf16[192,1024]{1,0:T(8,128)(2,1)}), bf16[192,8192]{1,0:T(8,128)(2,1)}) %all-gather.16.cloned.1.call-update) | async-done | bytes 3145744 | tf_op jit(solution)/shard_map/all_gather | solution.py:34
  397.1 23.1 %while.74 = (s32[]{:T(128)}, f32[2,96,1024]{2,1,0:T(8,128)S(1)}, bf16[2,96,8192]{2,1,0:T(8,128)(2,1)}, s32[2]{0:T(128)S(1)}, bf16[2,8192,1024]{2,1,0:T(8,128)(2,1)}, /*index=5*/s32[]{:T(128)}, s32[]{:T(128)}, s32[]{:T(128)}) while((s32[]{:T(128)}, f32[2,96,1024]{2,1,0:T(8,128)S(1)}, bf16[2,96,8192]{2,1,0:T(8,128)(2,1)}, s32[2]{0:T(128)S(1)}, ...), condition=%wide.region_37.40_spmd, body=%wide.region_36.39_spmd.sunk | while | flops 1610612736 | bytes 18744456 | solution.py:45
  399.6 9.0 %fusion.204 = f32[2,96,1024]{2,1,0:T(8,128)S(1)} fusion(f32[2,96,1024]{2,1,0:T(8,128)S(1)} %get-tuple-element.678, s32[]{:T(128)} %get-tuple-element.677, bf16[2,8192,1024]{2,1,0:T(8,128)(2,1)} %get-tuple-element.689, s32[]{:T(128)S(6)} %select_n.657, bf16[2,96,8192]{2,1,0:T(8,128)(2,1)} %get-tuple-element.687), kind=kOutput, calls=%fused_computation.66.clone.1 | convolution fusion | flops 1610612736 | bytes 18744324 | tf_op jit(solution)/shard_map/while/body/eval_jaxpr/dot_general | solution.py:43
  411.2 9.0 %fusion.204 = f32[2,96,1024]{2,1,0:T(8,128)S(1)} fusion(f32[2,96,1024]{2,1,0:T(8,128)S(1)} %get-tuple-element.678, s32[]{:T(128)} %get-tuple-element.677, bf16[2,8192,1024]{2,1,0:T(8,128)(2,1)} %get-tuple-element.689, s32[]{:T(128)S(6)} %select_n.657, bf16[2,96,8192]{2,1,0:T(8,128)(2,1)} %get-tuple-element.687), kind=kOutput, calls=%fused_computation.66.clone.1 | convolution fusion | flops 1610612736 | bytes 18744324 | tf_op jit(solution)/shard_map/while/body/eval_jaxpr/dot_general | solution.py:43
  421.2 14.8 %pmax.53 = f32[96]{0:T(128)S(1)} all-reduce(f32[96]{0:T(128)S(1)} %abs_reduce_fusion.2), channel_id=1, replica_groups=mesh['segment'=4,'col'=8] {'col'}, use_global_device_ids=true, to_apply=%region_39.42 | all-reduce | flops 96 | bytes 768 | tf_op jit(solution)/shard_map/pmax | solution.py:48
  436.2 3.4 collective-permute-start.4
  439.6 3.1 collective-permute-done.4
  447.8 34.4 %all-gather.18.cloned.1.call-done = bf16[192,8192]{1,0:T(8,128)(2,1)} async-done(((bf16[192,1024]{1,0:T(8,128)(2,1)}), bf16[192,8192]{1,0:T(8,128)(2,1)}) %all-gather.18.cloned.1.call-update) | async-done | bytes 3145744 | tf_op jit(solution)/shard_map/all_gather | solution.py:34
  482.4 23.1 %while.75 = (s32[]{:T(128)}, f32[2,96,1024]{2,1,0:T(8,128)S(1)}, bf16[2,96,8192]{2,1,0:T(8,128)(2,1)}, s32[2]{0:T(128)S(1)}, bf16[2,8192,1024]{2,1,0:T(8,128)(2,1)}, /*index=5*/s32[]{:T(128)}, s32[]{:T(128)}, s32[]{:T(128)}) while((s32[]{:T(128)}, f32[2,96,1024]{2,1,0:T(8,128)S(1)}, bf16[2,96,8192]{2,1,0:T(8,128)(2,1)}, s32[2]{0:T(128)S(1)}, ...), condition=%wide.region_45.48_spmd, body=%wide.region_44.47_spmd.sunk | while | flops 1610612736 | bytes 18744456 | solution.py:45
  484.9 9.0 %fusion.207 = f32[2,96,1024]{2,1,0:T(8,128)S(1)} fusion(f32[2,96,1024]{2,1,0:T(8,128)S(1)} %get-tuple-element.702, s32[]{:T(128)} %get-tuple-element.701, bf16[2,8192,1024]{2,1,0:T(8,128)(2,1)} %get-tuple-element.713, s32[]{:T(128)S(6)} %select_n.658, bf16[2,96,8192]{2,1,0:T(8,128)(2,1)} %get-tuple-element.711), kind=kOutput, calls=%fused_computation.74.clone.1 | convolution fusion | flops 1610612736 | bytes 18744324 | tf_op jit(solution)/shard_map/while/body/eval_jaxpr/dot_general | solution.py:43
  496.5 9.0 %fusion.207 = f32[2,96,1024]{2,1,0:T(8,128)S(1)} fusion(f32[2,96,1024]{2,1,0:T(8,128)S(1)} %get-tuple-element.702, s32[]{:T(128)} %get-tuple-element.701, bf16[2,8192,1024]{2,1,0:T(8,128)(2,1)} %get-tuple-element.713, s32[]{:T(128)S(6)} %select_n.658, bf16[2,96,8192]{2,1,0:T(8,128)(2,1)} %get-tuple-element.711), kind=kOutput, calls=%fused_computation.74.clone.1 | convolution fusion | flops 1610612736 | bytes 18744324 | tf_op jit(solution)/shard_map/while/body/eval_jaxpr/dot_general | solution.py:43
  506.5 14.7 %pmax.54 = f32[96]{0:T(128)S(1)} all-reduce(f32[96]{0:T(128)S(1)} %abs_reduce_fusion.1), channel_id=1, replica_groups=mesh['segment'=4,'col'=8] {'col'}, use_global_device_ids=true, to_apply=%region_47.50 | all-reduce | flops 96 | bytes 768 | tf_op jit(solution)/shard_map/pmax | solution.py:48
  521.5 3.4 collective-permute-start.5
  524.9 3.1 collective-permute-done.5
  530.1 37.4 %all-gather.20.cloned.1.call-done = bf16[192,8192]{1,0:T(8,128)(2,1)} async-done(((bf16[192,1024]{1,0:T(8,128)(2,1)}), bf16[192,8192]{1,0:T(8,128)(2,1)}) %all-gather.20.cloned.1.call-update) | async-done | bytes 3145744 | tf_op jit(solution)/shard_map/all_gather | solution.py:34
  567.6 23.1 %while.76 = (s32[]{:T(128)}, f32[2,96,1024]{2,1,0:T(8,128)S(1)}, bf16[2,96,8192]{2,1,0:T(8,128)(2,1)}, s32[2]{0:T(128)S(1)}, bf16[2,8192,1024]{2,1,0:T(8,128)(2,1)}, /*index=5*/s32[]{:T(128)}, s32[]{:T(128)}, s32[]{:T(128)}) while((s32[]{:T(128)}, f32[2,96,1024]{2,1,0:T(8,128)S(1)}, bf16[2,96,8192]{2,1,0:T(8,128)(2,1)}, s32[2]{0:T(128)S(1)}, ...), condition=%wide.region_53.56_spmd, body=%wide.region_52.55_spmd.sunk | while | flops 1610612736 | bytes 18744456 | solution.py:45
  570.2 9.0 %fusion.210 = f32[2,96,1024]{2,1,0:T(8,128)S(1)} fusion(f32[2,96,1024]{2,1,0:T(8,128)S(1)} %get-tuple-element.726, s32[]{:T(128)} %get-tuple-element.725, bf16[2,8192,1024]{2,1,0:T(8,128)(2,1)} %get-tuple-element.737, s32[]{:T(128)S(6)} %select_n.659, bf16[2,96,8192]{2,1,0:T(8,128)(2,1)} %get-tuple-element.735), kind=kOutput, calls=%fused_computation.82.clone.1 | convolution fusion | flops 1610612736 | bytes 18744324 | tf_op jit(solution)/shard_map/while/body/eval_jaxpr/dot_general | solution.py:43
  581.8 9.0 %fusion.210 = f32[2,96,1024]{2,1,0:T(8,128)S(1)} fusion(f32[2,96,1024]{2,1,0:T(8,128)S(1)} %get-tuple-element.726, s32[]{:T(128)} %get-tuple-element.725, bf16[2,8192,1024]{2,1,0:T(8,128)(2,1)} %get-tuple-element.737, s32[]{:T(128)S(6)} %select_n.659, bf16[2,96,8192]{2,1,0:T(8,128)(2,1)} %get-tuple-element.735), kind=kOutput, calls=%fused_computation.82.clone.1 | convolution fusion | flops 1610612736 | bytes 18744324 | tf_op jit(solution)/shard_map/while/body/eval_jaxpr/dot_general | solution.py:43
  591.7 14.8 %pmax.55 = f32[96]{0:T(128)S(1)} all-reduce(f32[96]{0:T(128)S(1)} %abs_reduce_fusion), channel_id=1, replica_groups=mesh['segment'=4,'col'=8] {'col'}, use_global_device_ids=true, to_apply=%region_55.58 | all-reduce | flops 96 | bytes 768 | tf_op jit(solution)/shard_map/pmax | solution.py:48
  (184 shorter events, 49.9 us)
Async XLA Ops:
  7.2 48.7 %all-gather.8.cloned.1.call-start = ((), (), s32[]{:S(2)}) async-start(), calls=%async_computation | async-start | bytes 3538944 | tf_op jit(solution)/shard_map/all_gather | solution.py:34
  14.7 126.4 %all-gather.10.cloned.1.call-start = ((), (), s32[]{:S(2)}) async-start(), calls=%async_computation.1 | async-start | bytes 3538944 | tf_op jit(solution)/shard_map/all_gather | solution.py:34
  79.1 22.6 %copy-start = (bf16[384,1024]{1,0:T(8,128)(2,1)S(1)}, bf16[384,1024]{1,0:T(8,128)(2,1)}, u32[]{:S(2)}) copy-start(bf16[384,1024]{1,0:T(8,128)(2,1)} %param.21) | copy-start | bytes 2359300
  95.1 6.6 %collective-permute-start = (bf16[96,1024]{1,0:T(8,128)(2,1)S(1)}, bf16[96,1024]{1,0:T(8,128)(2,1)S(1)}, u32[]{:S(2)}, u32[]{:S(2)}) collective-permute-start(bf16[96,1024]{1,0:T(8,128)(2,1)S(1)} %get-tuple-element.319), channel_id=1, source_target_pairs={{0,8},{8,16},{16,24},{1,9},{9,17},{17,25},{2,10},{10,18},{18,26},{... | collective-permute-start | bytes 589832 | tf_op jit(solution)/shard_map/ppermute | solution.py:13
  103.7 122.8 %all-gather.12.cloned.1.call-start = ((), (), s32[]{:S(2)}) async-start(), calls=%async_computation.2 | async-start | bytes 3538944 | tf_op jit(solution)/shard_map/all_gather | solution.py:34
  180.4 6.6 %collective-permute-start.1 = (bf16[96,1024]{1,0:T(8,128)(2,1)S(1)}, bf16[96,1024]{1,0:T(8,128)(2,1)S(1)}, u32[]{:S(2)}, u32[]{:S(2)}) collective-permute-start(bf16[96,1024]{1,0:T(8,128)(2,1)S(1)} %get-tuple-element.313), channel_id=1, source_target_pairs={{0,8},{8,16},{16,24},{1,9},{9,17},{17,25},{2,10},{10,18},{18,26},{... | collective-permute-start | bytes 589832 | tf_op jit(solution)/shard_map/ppermute | solution.py:13
  188.9 122.8 %all-gather.14.cloned.1.call-start = ((), (), s32[]{:S(2)}) async-start(), calls=%async_computation.3 | async-start | bytes 3538944 | tf_op jit(solution)/shard_map/all_gather | solution.py:34
  265.7 6.6 %collective-permute-start.2 = (bf16[96,1024]{1,0:T(8,128)(2,1)S(1)}, bf16[96,1024]{1,0:T(8,128)(2,1)S(1)}, u32[]{:S(2)}, u32[]{:S(2)}) collective-permute-start(bf16[96,1024]{1,0:T(8,128)(2,1)S(1)} %get-tuple-element.307), channel_id=1, source_target_pairs={{0,8},{8,16},{16,24},{1,9},{9,17},{17,25},{2,10},{10,18},{18,26},{... | collective-permute-start | bytes 589832 | tf_op jit(solution)/shard_map/ppermute | solution.py:13
  274.2 122.8 %all-gather.16.cloned.1.call-start = ((), (), s32[]{:S(2)}) async-start(), calls=%async_computation.4 | async-start | bytes 3538944 | tf_op jit(solution)/shard_map/all_gather | solution.py:34
  351.0 6.6 %collective-permute-start.3 = (bf16[96,1024]{1,0:T(8,128)(2,1)S(1)}, bf16[96,1024]{1,0:T(8,128)(2,1)S(1)}, u32[]{:S(2)}, u32[]{:S(2)}) collective-permute-start(bf16[96,1024]{1,0:T(8,128)(2,1)S(1)} %get-tuple-element.301), channel_id=1, source_target_pairs={{0,8},{8,16},{16,24},{1,9},{9,17},{17,25},{2,10},{10,18},{18,26},{... | collective-permute-start | bytes 589832 | tf_op jit(solution)/shard_map/ppermute | solution.py:13
  359.5 122.8 %all-gather.18.cloned.1.call-start = ((), (), s32[]{:S(2)}) async-start(), calls=%async_computation.5 | async-start | bytes 3538944 | tf_op jit(solution)/shard_map/all_gather | solution.py:34
  436.2 6.5 %collective-permute-start.4 = (bf16[96,1024]{1,0:T(8,128)(2,1)S(1)}, bf16[96,1024]{1,0:T(8,128)(2,1)S(1)}, u32[]{:S(2)}, u32[]{:S(2)}) collective-permute-start(bf16[96,1024]{1,0:T(8,128)(2,1)S(1)} %get-tuple-element.295), channel_id=1, source_target_pairs={{0,8},{8,16},{16,24},{1,9},{9,17},{17,25},{2,10},{10,18},{18,26},{... | collective-permute-start | bytes 589832 | tf_op jit(solution)/shard_map/ppermute | solution.py:13
  444.8 122.8 %all-gather.20.cloned.1.call-start = ((), (), s32[]{:S(2)}) async-start(), calls=%async_computation.6 | async-start | bytes 3538944 | tf_op jit(solution)/shard_map/all_gather | solution.py:34
  521.5 6.6 %collective-permute-start.5 = (bf16[96,1024]{1,0:T(8,128)(2,1)S(1)}, bf16[96,1024]{1,0:T(8,128)(2,1)S(1)}, u32[]{:S(2)}, u32[]{:S(2)}) collective-permute-start(bf16[96,1024]{1,0:T(8,128)(2,1)S(1)} %get-tuple-element.289), channel_id=1, source_target_pairs={{0,8},{8,16},{16,24},{1,9},{9,17},{17,25},{2,10},{10,18},{18,26},{... | collective-permute-start | bytes 589832 | tf_op jit(solution)/shard_map/ppermute | solution.py:13
  606.7 0.6 copy-start.2
  607.3 0.9 copy-start.1
Sparse Core Ops, SparseCore 0:
  14.9 40.9 all-gather.7
  103.8 37.3 all-gather.9
  189.1 37.3 all-gather.11
  274.3 37.3 all-gather.13
  359.6 37.3 all-gather.15
  444.9 37.3 all-gather.17
  530.2 37.3 all-gather.19
where the time goes:
time: 616 us; the launch traced here: 615 us
  waiting for transfers between devices  266 us (43%)
  matrix products  126 us (20%)
  blocking collectives  103 us (17%)
  local copies, waits for them, and re-layouts  36 us (6%)
  loops' own time  27.4 us (4%)
  starting transfers between devices  20.8 us (3%)
  between operations  19.5 us (3%)
  other arithmetic  15.2 us (2%)
    all_gather x7, waiting for transfers between devices, advance(): gathered_piece = lax.all_gather(arranged_in, 'col', axis=1, tiled=True)  248 us
    dot_general x14, matrix products, one_block(): return jnp.dot(rows_block, weight_block, preferred_element_type=jnp.float32)  126 us
    pmax x7, blocking collectives, advance(): maximum = lax.pmax(jnp.max(jnp.abs(chosen), axis=1), 'col') + epsilon  103 us
    another operation x7, loops' own time, advance(): result = lax.map(one_block, (pieces, block_bit))  27.4 us
    ppermute x6, starting transfers between devices, passed_along(): return lax.ppermute(value, axis, pairs)  20.5 us
    ppermute x6, waiting for transfers between devices, passed_along(): return lax.ppermute(value, axis, pairs)  18.7 us
  transfers between devices with their start and end apart: 13, of which 13 were waited for; matrix products, arithmetic and copies ran while one was open for 2% of the time, Pallas kernels for 0%

commit v1 on v0

--- a/solution.py
+++ b/solution.py
@@ -31,7 +31,7 @@
     arranged_in = jnp.where(
         filled[:, None], jnp.take(vector, source, axis=0), jnp.zeros((), vector.dtype)
     )
-    gathered_piece = lax.all_gather(arranged_in, "col", axis=1, tiled=True)
+    gathered_piece = jnp.concatenate(lax.all_gather(arranged_in, "col"), axis=1)
     width = gathered_piece.shape[1]
     pieces = gathered_piece.reshape(block_count, block, width)
 

time: 616 us -> 724 us (1.18); the launches traced: 615 us -> 714 us
  local copies, waits for them, and re-layouts: 36 us -> 120 us
  other arithmetic: 15.2 us -> 29.3 us
    reshape x0 -> x7, local copies, waits for them, and re-layouts: none -> 37.2 us  [advance(): gathered_piece = jnp.concatenate(lax.all_gather(arranged_in, 'col'), axis=1)]
    another operation x8 -> x15, local copies, waits for them, and re-layouts: 0.52 us -> 36.2 us  [the longest x7 29.4 us: advance(): pieces = gathered_piece.reshape(block_count, block, width)]
    gather x7, local copies, waits for them, and re-layouts: 5.17 us -> 14.4 us  [advance(): chosen = jnp.take(arranged_out, slot, axis=0)]
    dynamic_update_slice x7, other arithmetic: 1.02 us -> 9.05 us  [local(): lax.dynamic_update_slice_in_dim(env_out, jnp.where(active, current, old_e...]
where the time goes in v1:
time: 724 us; the launch traced here: 714 us
  waiting for transfers between devices  265 us (37%)
  matrix products  130 us (18%)
  local copies, waits for them, and re-layouts  120 us (17%)
  blocking collectives  103 us (14%)
  other arithmetic  29.3 us (4%)
  loops' own time  26.9 us (4%)
  starting transfers between devices  20.5 us (3%)
  between operations  19.7 us (3%)
    all_gather x7, waiting for transfers between devices, advance(): gathered_piece = jnp.concatenate(lax.all_gather(arranged_in, 'col'), axis=1)  246 us
    dot_general x14, matrix products, one_block(): return jnp.dot(rows_block, weight_block, preferred_element_type=jnp.float32)  130 us
    pmax x7, blocking collectives, advance(): maximum = lax.pmax(jnp.max(jnp.abs(chosen), axis=1), 'col') + epsilon  103 us
    reshape x7, local copies, waits for them, and re-layouts, advance(): gathered_piece = jnp.concatenate(lax.all_gather(arranged_in, 'col'), axis=1)  37.2 us
    another operation x7, local copies, waits for them, and re-layouts, advance(): pieces = gathered_piece.reshape(block_count, block, width)  29.4 us
    another operation x7, loops' own time, advance(): result = lax.map(one_block, (pieces, block_bit))  26.9 us
    ppermute x6, starting transfers between devices, passed_along(): return lax.ppermute(value, axis, pairs)  20.3 us
    ppermute x6, waiting for transfers between devices, passed_along(): return lax.ppermute(value, axis, pairs)  18.9 us
  transfers between devices with their start and end apart: 13, of which 13 were waited for; matrix products, arithmetic and copies ran while one was open for 2% of the time, Pallas kernels for 0%

profile of v1, /device:TPU:0, one launch (start us, length us, event | category | flops | bytes accessed | tf_op | source)
XLA Modules:
  0.0 714.1 jit_solution(738800555042794962)
XLA Ops:
  18.2 38.2 %all-gather.15.cloned.1.call-done = bf16[1536,1024]{1,0:T(8,128)(2,1)} async-done(((bf16[192,1024]{1,0:T(8,128)(2,1)}), bf16[1536,1024]{1,0:T(8,128)(2,1)}) %all-gather.15.cloned.1.call-update) | async-done | bytes 3145744 | tf_op jit(solution)/shard_map/all_gather | solution.py:34
  56.4 5.3 copy.20
  61.7 4.2 reshape_reshape.21
  66.9 24.1 %while.70 = (s32[]{:T(128)}, f32[2,96,1024]{2,1,0:T(8,128)}, bf16[2,96,8192]{2,1,0:T(8,128)(2,1)S(1)}, s32[2]{0:T(128)S(1)}, bf16[2,8192,1024]{2,1,0:T(8,128)(2,1)}, /*index=5*/s32[]{:T(128)}, s32[]{:T(128)}, s32[]{:T(128)}) while((s32[]{:T(128)}, f32[2,96,1024]{2,1,0:T(8,128)}, bf16[2,96,8192]{2,1,0:T(8,128)(2,1)S(1)}, s32[2]{0:T(128)S(1)}, ...), condition=%wide.region_5.7_spmd, body=%wide.region_4.6_spmd.sunk | while | flops 1610612736 | bytes 18744456 | solution.py:45
  69.6 9.3 %fusion.192 = f32[2,96,1024]{2,1,0:T(8,128)} fusion(f32[2,96,1024]{2,1,0:T(8,128)} %get-tuple-element.582, s32[]{:T(128)} %get-tuple-element.581, bf16[2,8192,1024]{2,1,0:T(8,128)(2,1)} %get-tuple-element.593, s32[]{:T(128)S(6)} %select_n.653, bf16[2,96,8192]{2,1,0:T(8,128)(2,1)S(1)} %get-tuple-element.591), kind=kOutput, calls=%fused_computation.34.clone.1 | convolution fusion | flops 1610612736 | bytes 18744324 | tf_op jit(solution)/shard_map/while/body/eval_jaxpr/dot_general | solution.py:43
  81.7 9.3 %fusion.192 = f32[2,96,1024]{2,1,0:T(8,128)} fusion(f32[2,96,1024]{2,1,0:T(8,128)} %get-tuple-element.582, s32[]{:T(128)} %get-tuple-element.581, bf16[2,8192,1024]{2,1,0:T(8,128)(2,1)} %get-tuple-element.593, s32[]{:T(128)S(6)} %select_n.653, bf16[2,96,8192]{2,1,0:T(8,128)(2,1)S(1)} %get-tuple-element.591), kind=kOutput, calls=%fused_computation.34.clone.1 | convolution fusion | flops 1610612736 | bytes 18744324 | tf_op jit(solution)/shard_map/while/body/eval_jaxpr/dot_general | solution.py:43
  93.2 14.7 %pmax.49 = f32[96]{0:T(128)S(1)} all-reduce(f32[96]{0:T(128)S(1)} %abs_reduce_fusion.6), channel_id=1, replica_groups=mesh['segment'=4,'col'=8] {'col'}, use_global_device_ids=true, to_apply=%region_7.10 | all-reduce | flops 96 | bytes 768 | tf_op jit(solution)/shard_map/pmax | solution.py:48
  121.2 34.1 %all-gather.17.cloned.1.call-done = bf16[1536,1024]{1,0:T(8,128)(2,1)} async-done(((bf16[192,1024]{1,0:T(8,128)(2,1)}), bf16[1536,1024]{1,0:T(8,128)(2,1)}) %all-gather.17.cloned.1.call-update) | async-done | bytes 3145744 | tf_op jit(solution)/shard_map/all_gather | solution.py:34
  155.3 5.3 copy.22
  160.6 4.2 reshape_reshape.22
  165.8 23.7 %while.71 = (s32[]{:T(128)}, f32[2,96,1024]{2,1,0:T(8,128)}, bf16[2,96,8192]{2,1,0:T(8,128)(2,1)S(1)}, s32[2]{0:T(128)S(1)}, bf16[2,8192,1024]{2,1,0:T(8,128)(2,1)}, /*index=5*/s32[]{:T(128)}, s32[]{:T(128)}, s32[]{:T(128)}) while((s32[]{:T(128)}, f32[2,96,1024]{2,1,0:T(8,128)}, bf16[2,96,8192]{2,1,0:T(8,128)(2,1)S(1)}, s32[2]{0:T(128)S(1)}, ...), condition=%wide.region_13.16_spmd, body=%wide.region_12.15_spmd.sunk | while | flops 1610612736 | bytes 18744456 | solution.py:45
  168.3 9.3 %fusion.195 = f32[2,96,1024]{2,1,0:T(8,128)} fusion(f32[2,96,1024]{2,1,0:T(8,128)} %get-tuple-element.606, s32[]{:T(128)} %get-tuple-element.605, bf16[2,8192,1024]{2,1,0:T(8,128)(2,1)} %get-tuple-element.617, s32[]{:T(128)S(6)} %select_n.654, bf16[2,96,8192]{2,1,0:T(8,128)(2,1)S(1)} %get-tuple-element.615), kind=kOutput, calls=%fused_computation.42.clone.1 | convolution fusion | flops 1610612736 | bytes 18744324 | tf_op jit(solution)/shard_map/while/body/eval_jaxpr/dot_general | solution.py:43
  180.1 9.3 %fusion.195 = f32[2,96,1024]{2,1,0:T(8,128)} fusion(f32[2,96,1024]{2,1,0:T(8,128)} %get-tuple-element.606, s32[]{:T(128)} %get-tuple-element.605, bf16[2,8192,1024]{2,1,0:T(8,128)(2,1)} %get-tuple-element.617, s32[]{:T(128)S(6)} %select_n.654, bf16[2,96,8192]{2,1,0:T(8,128)(2,1)S(1)} %get-tuple-element.615), kind=kOutput, calls=%fused_computation.42.clone.1 | convolution fusion | flops 1610612736 | bytes 18744324 | tf_op jit(solution)/shard_map/while/body/eval_jaxpr/dot_general | solution.py:43
  191.7 14.8 %pmax.50 = f32[96]{0:T(128)S(1)} all-reduce(f32[96]{0:T(128)S(1)} %abs_reduce_fusion.5), channel_id=1, replica_groups=mesh['segment'=4,'col'=8] {'col'}, use_global_device_ids=true, to_apply=%region_15.18 | all-reduce | flops 96 | bytes 768 | tf_op jit(solution)/shard_map/pmax | solution.py:48
  220.8 34.5 %all-gather.19.cloned.1.call-done = bf16[1536,1024]{1,0:T(8,128)(2,1)} async-done(((bf16[192,1024]{1,0:T(8,128)(2,1)}), bf16[1536,1024]{1,0:T(8,128)(2,1)}) %all-gather.19.cloned.1.call-update) | async-done | bytes 3145744 | tf_op jit(solution)/shard_map/all_gather | solution.py:34
  255.3 5.3 copy.24
  260.6 4.2 reshape_reshape.23
  265.8 23.7 %while.72 = (s32[]{:T(128)}, f32[2,96,1024]{2,1,0:T(8,128)}, bf16[2,96,8192]{2,1,0:T(8,128)(2,1)S(1)}, s32[2]{0:T(128)S(1)}, bf16[2,8192,1024]{2,1,0:T(8,128)(2,1)}, /*index=5*/s32[]{:T(128)}, s32[]{:T(128)}, s32[]{:T(128)}) while((s32[]{:T(128)}, f32[2,96,1024]{2,1,0:T(8,128)}, bf16[2,96,8192]{2,1,0:T(8,128)(2,1)S(1)}, s32[2]{0:T(128)S(1)}, ...), condition=%wide.region_21.24_spmd, body=%wide.region_20.23_spmd.sunk | while | flops 1610612736 | bytes 18744456 | solution.py:45
  268.3 9.3 %fusion.198 = f32[2,96,1024]{2,1,0:T(8,128)} fusion(f32[2,96,1024]{2,1,0:T(8,128)} %get-tuple-element.630, s32[]{:T(128)} %get-tuple-element.629, bf16[2,8192,1024]{2,1,0:T(8,128)(2,1)} %get-tuple-element.641, s32[]{:T(128)S(6)} %select_n.655, bf16[2,96,8192]{2,1,0:T(8,128)(2,1)S(1)} %get-tuple-element.639), kind=kOutput, calls=%fused_computation.50.clone.1 | convolution fusion | flops 1610612736 | bytes 18744324 | tf_op jit(solution)/shard_map/while/body/eval_jaxpr/dot_general | solution.py:43
  280.2 9.3 %fusion.198 = f32[2,96,1024]{2,1,0:T(8,128)} fusion(f32[2,96,1024]{2,1,0:T(8,128)} %get-tuple-element.630, s32[]{:T(128)} %get-tuple-element.629, bf16[2,8192,1024]{2,1,0:T(8,128)(2,1)} %get-tuple-element.641, s32[]{:T(128)S(6)} %select_n.655, bf16[2,96,8192]{2,1,0:T(8,128)(2,1)S(1)} %get-tuple-element.639), kind=kOutput, calls=%fused_computation.50.clone.1 | convolution fusion | flops 1610612736 | bytes 18744324 | tf_op jit(solution)/shard_map/while/body/eval_jaxpr/dot_general | solution.py:43
  291.7 14.8 %pmax.51 = f32[96]{0:T(128)S(1)} all-reduce(f32[96]{0:T(128)S(1)} %abs_reduce_fusion.4), channel_id=1, replica_groups=mesh['segment'=4,'col'=8] {'col'}, use_global_device_ids=true, to_apply=%region_23.26 | all-reduce | flops 96 | bytes 768 | tf_op jit(solution)/shard_map/pmax | solution.py:48
  321.2 34.1 %all-gather.21.cloned.1.call-done = bf16[1536,1024]{1,0:T(8,128)(2,1)} async-done(((bf16[192,1024]{1,0:T(8,128)(2,1)}), bf16[1536,1024]{1,0:T(8,128)(2,1)}) %all-gather.21.cloned.1.call-update) | async-done | bytes 3145744 | tf_op jit(solution)/shard_map/all_gather | solution.py:34
  355.3 5.3 copy.26
  360.6 4.2 reshape_reshape.24
  365.8 23.7 %while.73 = (s32[]{:T(128)}, f32[2,96,1024]{2,1,0:T(8,128)}, bf16[2,96,8192]{2,1,0:T(8,128)(2,1)S(1)}, s32[2]{0:T(128)S(1)}, bf16[2,8192,1024]{2,1,0:T(8,128)(2,1)}, /*index=5*/s32[]{:T(128)}, s32[]{:T(128)}, s32[]{:T(128)}) while((s32[]{:T(128)}, f32[2,96,1024]{2,1,0:T(8,128)}, bf16[2,96,8192]{2,1,0:T(8,128)(2,1)S(1)}, s32[2]{0:T(128)S(1)}, ...), condition=%wide.region_29.32_spmd, body=%wide.region_28.31_spmd.sunk | while | flops 1610612736 | bytes 18744456 | solution.py:45
  368.3 9.3 %fusion.201 = f32[2,96,1024]{2,1,0:T(8,128)} fusion(f32[2,96,1024]{2,1,0:T(8,128)} %get-tuple-element.654, s32[]{:T(128)} %get-tuple-element.653, bf16[2,8192,1024]{2,1,0:T(8,128)(2,1)} %get-tuple-element.665, s32[]{:T(128)S(6)} %select_n.656, bf16[2,96,8192]{2,1,0:T(8,128)(2,1)S(1)} %get-tuple-element.663), kind=kOutput, calls=%fused_computation.58.clone.1 | convolution fusion | flops 1610612736 | bytes 18744324 | tf_op jit(solution)/shard_map/while/body/eval_jaxpr/dot_general | solution.py:43
  380.2 9.3 %fusion.201 = f32[2,96,1024]{2,1,0:T(8,128)} fusion(f32[2,96,1024]{2,1,0:T(8,128)} %get-tuple-element.654, s32[]{:T(128)} %get-tuple-element.653, bf16[2,8192,1024]{2,1,0:T(8,128)(2,1)} %get-tuple-element.665, s32[]{:T(128)S(6)} %select_n.656, bf16[2,96,8192]{2,1,0:T(8,128)(2,1)S(1)} %get-tuple-element.663), kind=kOutput, calls=%fused_computation.58.clone.1 | convolution fusion | flops 1610612736 | bytes 18744324 | tf_op jit(solution)/shard_map/while/body/eval_jaxpr/dot_general | solution.py:43
  391.7 14.7 %pmax.52 = f32[96]{0:T(128)S(1)} all-reduce(f32[96]{0:T(128)S(1)} %abs_reduce_fusion.3), channel_id=1, replica_groups=mesh['segment'=4,'col'=8] {'col'}, use_global_device_ids=true, to_apply=%region_31.34 | all-reduce | flops 96 | bytes 768 | tf_op jit(solution)/shard_map/pmax | solution.py:48
  421.2 34.1 %all-gather.23.cloned.1.call-done = bf16[1536,1024]{1,0:T(8,128)(2,1)} async-done(((bf16[192,1024]{1,0:T(8,128)(2,1)}), bf16[1536,1024]{1,0:T(8,128)(2,1)}) %all-gather.23.cloned.1.call-update) | async-done | bytes 3145744 | tf_op jit(solution)/shard_map/all_gather | solution.py:34
  455.3 5.3 copy.28
  460.6 4.2 reshape_reshape.25
  465.8 23.7 %while.74 = (s32[]{:T(128)}, f32[2,96,1024]{2,1,0:T(8,128)}, bf16[2,96,8192]{2,1,0:T(8,128)(2,1)S(1)}, s32[2]{0:T(128)S(1)}, bf16[2,8192,1024]{2,1,0:T(8,128)(2,1)}, /*index=5*/s32[]{:T(128)}, s32[]{:T(128)}, s32[]{:T(128)}) while((s32[]{:T(128)}, f32[2,96,1024]{2,1,0:T(8,128)}, bf16[2,96,8192]{2,1,0:T(8,128)(2,1)S(1)}, s32[2]{0:T(128)S(1)}, ...), condition=%wide.region_37.40_spmd, body=%wide.region_36.39_spmd.sunk | while | flops 1610612736 | bytes 18744456 | solution.py:45
  468.4 9.3 %fusion.204 = f32[2,96,1024]{2,1,0:T(8,128)} fusion(f32[2,96,1024]{2,1,0:T(8,128)} %get-tuple-element.678, s32[]{:T(128)} %get-tuple-element.677, bf16[2,8192,1024]{2,1,0:T(8,128)(2,1)} %get-tuple-element.689, s32[]{:T(128)S(6)} %select_n.657, bf16[2,96,8192]{2,1,0:T(8,128)(2,1)S(1)} %get-tuple-element.687), kind=kOutput, calls=%fused_computation.66.clone.1 | convolution fusion | flops 1610612736 | bytes 18744324 | tf_op jit(solution)/shard_map/while/body/eval_jaxpr/dot_general | solution.py:43
  480.2 9.3 %fusion.204 = f32[2,96,1024]{2,1,0:T(8,128)} fusion(f32[2,96,1024]{2,1,0:T(8,128)} %get-tuple-element.678, s32[]{:T(128)} %get-tuple-element.677, bf16[2,8192,1024]{2,1,0:T(8,128)(2,1)} %get-tuple-element.689, s32[]{:T(128)S(6)} %select_n.657, bf16[2,96,8192]{2,1,0:T(8,128)(2,1)S(1)} %get-tuple-element.687), kind=kOutput, calls=%fused_computation.66.clone.1 | convolution fusion | flops 1610612736 | bytes 18744324 | tf_op jit(solution)/shard_map/while/body/eval_jaxpr/dot_general | solution.py:43
  491.7 14.7 %pmax.53 = f32[96]{0:T(128)S(1)} all-reduce(f32[96]{0:T(128)S(1)} %abs_reduce_fusion.2), channel_id=1, replica_groups=mesh['segment'=4,'col'=8] {'col'}, use_global_device_ids=true, to_apply=%region_39.42 | all-reduce | flops 96 | bytes 768 | tf_op jit(solution)/shard_map/pmax | solution.py:48
  521.1 34.2 %all-gather.25.cloned.1.call-done = bf16[1536,1024]{1,0:T(8,128)(2,1)} async-done(((bf16[192,1024]{1,0:T(8,128)(2,1)}), bf16[1536,1024]{1,0:T(8,128)(2,1)}) %all-gather.25.cloned.1.call-update) | async-done | bytes 3145744 | tf_op jit(solution)/shard_map/all_gather | solution.py:34
  555.4 5.3 copy.30
  560.7 4.2 reshape_reshape.26
  565.8 23.7 %while.75 = (s32[]{:T(128)}, f32[2,96,1024]{2,1,0:T(8,128)}, bf16[2,96,8192]{2,1,0:T(8,128)(2,1)S(1)}, s32[2]{0:T(128)S(1)}, bf16[2,8192,1024]{2,1,0:T(8,128)(2,1)}, /*index=5*/s32[]{:T(128)}, s32[]{:T(128)}, s32[]{:T(128)}) while((s32[]{:T(128)}, f32[2,96,1024]{2,1,0:T(8,128)}, bf16[2,96,8192]{2,1,0:T(8,128)(2,1)S(1)}, s32[2]{0:T(128)S(1)}, ...), condition=%wide.region_45.48_spmd, body=%wide.region_44.47_spmd.sunk | while | flops 1610612736 | bytes 18744456 | solution.py:45
  568.4 9.3 %fusion.207 = f32[2,96,1024]{2,1,0:T(8,128)} fusion(f32[2,96,1024]{2,1,0:T(8,128)} %get-tuple-element.702, s32[]{:T(128)} %get-tuple-element.701, bf16[2,8192,1024]{2,1,0:T(8,128)(2,1)} %get-tuple-element.713, s32[]{:T(128)S(6)} %select_n.658, bf16[2,96,8192]{2,1,0:T(8,128)(2,1)S(1)} %get-tuple-element.711), kind=kOutput, calls=%fused_computation.74.clone.1 | convolution fusion | flops 1610612736 | bytes 18744324 | tf_op jit(solution)/shard_map/while/body/eval_jaxpr/dot_general | solution.py:43
  580.2 9.3 %fusion.207 = f32[2,96,1024]{2,1,0:T(8,128)} fusion(f32[2,96,1024]{2,1,0:T(8,128)} %get-tuple-element.702, s32[]{:T(128)} %get-tuple-element.701, bf16[2,8192,1024]{2,1,0:T(8,128)(2,1)} %get-tuple-element.713, s32[]{:T(128)S(6)} %select_n.658, bf16[2,96,8192]{2,1,0:T(8,128)(2,1)S(1)} %get-tuple-element.711), kind=kOutput, calls=%fused_computation.74.clone.1 | convolution fusion | flops 1610612736 | bytes 18744324 | tf_op jit(solution)/shard_map/while/body/eval_jaxpr/dot_general | solution.py:43
  591.8 14.8 %pmax.54 = f32[96]{0:T(128)S(1)} all-reduce(f32[96]{0:T(128)S(1)} %abs_reduce_fusion.1), channel_id=1, replica_groups=mesh['segment'=4,'col'=8] {'col'}, use_global_device_ids=true, to_apply=%region_47.50 | all-reduce | flops 96 | bytes 768 | tf_op jit(solution)/shard_map/pmax | solution.py:48
  617.3 36.6 %all-gather.27.cloned.1.call-done = bf16[1536,1024]{1,0:T(8,128)(2,1)} async-done(((bf16[192,1024]{1,0:T(8,128)(2,1)}), bf16[1536,1024]{1,0:T(8,128)(2,1)}) %all-gather.27.cloned.1.call-update) | async-done | bytes 3145744 | tf_op jit(solution)/shard_map/all_gather | solution.py:34
  653.9 5.3 copy.32
  664.4 23.7 %while.76 = (s32[]{:T(128)}, f32[2,96,1024]{2,1,0:T(8,128)}, bf16[2,96,8192]{2,1,0:T(8,128)(2,1)S(1)}, s32[2]{0:T(128)S(1)}, bf16[2,8192,1024]{2,1,0:T(8,128)(2,1)}, /*index=5*/s32[]{:T(128)}, s32[]{:T(128)}, s32[]{:T(128)}) while((s32[]{:T(128)}, f32[2,96,1024]{2,1,0:T(8,128)}, bf16[2,96,8192]{2,1,0:T(8,128)(2,1)S(1)}, s32[2]{0:T(128)S(1)}, ...), condition=%wide.region_53.56_spmd, body=%wide.region_52.55_spmd.sunk | while | flops 1610612736 | bytes 18744456 | solution.py:45
  666.9 9.3 %fusion.210 = f32[2,96,1024]{2,1,0:T(8,128)} fusion(f32[2,96,1024]{2,1,0:T(8,128)} %get-tuple-element.726, s32[]{:T(128)} %get-tuple-element.725, bf16[2,8192,1024]{2,1,0:T(8,128)(2,1)} %get-tuple-element.737, s32[]{:T(128)S(6)} %select_n.659, bf16[2,96,8192]{2,1,0:T(8,128)(2,1)S(1)} %get-tuple-element.735), kind=kOutput, calls=%fused_computation.82.clone.1 | convolution fusion | flops 1610612736 | bytes 18744324 | tf_op jit(solution)/shard_map/while/body/eval_jaxpr/dot_general | solution.py:43
  678.7 9.3 %fusion.210 = f32[2,96,1024]{2,1,0:T(8,128)} fusion(f32[2,96,1024]{2,1,0:T(8,128)} %get-tuple-element.726, s32[]{:T(128)} %get-tuple-element.725, bf16[2,8192,1024]{2,1,0:T(8,128)(2,1)} %get-tuple-element.737, s32[]{:T(128)S(6)} %select_n.659, bf16[2,96,8192]{2,1,0:T(8,128)(2,1)S(1)} %get-tuple-element.735), kind=kOutput, calls=%fused_computation.82.clone.1 | convolution fusion | flops 1610612736 | bytes 18744324 | tf_op jit(solution)/shard_map/while/body/eval_jaxpr/dot_general | solution.py:43
  690.3 14.7 %pmax.55 = f32[96]{0:T(128)S(1)} all-reduce(f32[96]{0:T(128)S(1)} %abs_reduce_fusion), channel_id=1, replica_groups=mesh['segment'=4,'col'=8] {'col'}, use_global_device_ids=true, to_apply=%region_55.58 | all-reduce | flops 96 | bytes 768 | tf_op jit(solution)/shard_map/pmax | solution.py:48
  (202 shorter events, 126.0 us)
Async XLA Ops:
  7.2 49.3 %all-gather.15.cloned.1.call-start = ((), (), s32[]{:S(2)}) async-start(), calls=%async_computation | async-start | bytes 3538944 | tf_op jit(solution)/shard_map/all_gather | solution.py:34
  15.3 140.0 %all-gather.17.cloned.1.call-start = ((), (), s32[]{:S(2)}) async-start(), calls=%async_computation.1 | async-start | bytes 3538944 | tf_op jit(solution)/shard_map/all_gather | solution.py:34
  108.3 3.4 copy-start
  108.3 6.6 collective-permute-start
  117.8 137.5 %all-gather.19.cloned.1.call-start = ((), (), s32[]{:S(2)}) async-start(), calls=%async_computation.2 | async-start | bytes 3538944 | tf_op jit(solution)/shard_map/all_gather | solution.py:34
  208.3 6.5 collective-permute-start.1
  217.8 137.5 %all-gather.21.cloned.1.call-start = ((), (), s32[]{:S(2)}) async-start(), calls=%async_computation.3 | async-start | bytes 3538944 | tf_op jit(solution)/shard_map/all_gather | solution.py:34
  308.4 6.5 collective-permute-start.2
  317.8 137.5 %all-gather.23.cloned.1.call-start = ((), (), s32[]{:S(2)}) async-start(), calls=%async_computation.4 | async-start | bytes 3538944 | tf_op jit(solution)/shard_map/all_gather | solution.py:34
  408.4 6.5 collective-permute-start.3
  417.8 137.5 %all-gather.25.cloned.1.call-start = ((), (), s32[]{:S(2)}) async-start(), calls=%async_computation.5 | async-start | bytes 3538944 | tf_op jit(solution)/shard_map/all_gather | solution.py:34
  506.6 11.8 %copy-start.3 = (s32[96,1]{0,1:T(1,128)S(1)}, s32[96,1]{0,1:T(1,128)}, u32[]{:S(2)}) copy-start(s32[96,1]{0,1:T(1,128)} %get-tuple-element.287) | copy-start | bytes 1156
  508.4 6.5 collective-permute-start.4
  517.8 136.0 %all-gather.27.cloned.1.call-start = ((), (), s32[]{:S(2)}) async-start(), calls=%async_computation.6 | async-start | bytes 3538944 | tf_op jit(solution)/shard_map/all_gather | solution.py:34
  589.5 17.2 %copy-start.1 = (bf16[384,1024]{1,0:T(8,128)(2,1)S(1)}, bf16[384,1024]{1,0:T(8,128)(2,1)}, u32[]{:S(2)}) copy-start(bf16[384,1024]{1,0:T(8,128)(2,1)} %get-tuple-element.294) | copy-start | bytes 2359300
  606.9 47.0 %copy-start.2 = (bf16[384,1024]{1,0:T(8,128)(2,1)}, bf16[384,1024]{1,0:T(8,128)(2,1)S(1)}, u32[]{:S(2)}) copy-start(bf16[384,1024]{1,0:T(8,128)(2,1)S(1)} %get-tuple-element.288) | copy-start | bytes 2359300
  606.9 6.5 collective-permute-start.5
  705.3 1.8 copy-start.4
Sparse Core Ops, SparseCore 0:
  15.4 40.9 all-gather.14
  117.9 37.3 all-gather.16
  217.9 37.3 all-gather.18
  317.9 37.3 all-gather.20
  417.9 37.3 all-gather.22
  517.9 37.3 all-gather.24
  616.5 37.3 all-gather.26
